TPU v7x, 256 devices: a whole 4x4x8 slice. The times are simulated.
256 devices in a mesh: section: 8 (over z), seq: 32 (over y, x, core).
Axes of the slice: x: 4, y: 4, z: 8, core: 2. Of those that a mesh axis runs over, the one named last changes fastest.
Arguments:
- stream_in: bfloat16 [2, 4096, 4096], P(None, 'seq'), may hold values from -30 to 30
- norm_gain: float32 [8, 4096], P('section'), may hold values from 0.25 to 1.75
- proj_weight: bfloat16 [8, 32, 4, 128, 128], P('section'), may hold values from -0.5 to 0.5
Outputs:
- streams: bfloat16 [8, 2, 4096, 4096], P('section', None, 'seq')
All inputs are finite; a program needn't handle non-finite values.
Results may differ from a plain program's by a relative error of at most 0.014.
Values may be sent and summed in bfloat16 or wider, within the bound.
No kernel may reach another device: no remote copies, remote signals or barrier semaphores. Data moves between devices by JAX's collectives and lax.ppermute only.
A program may use at most 64 MiB of HBM per device.

v0:
```python
import jax
import jax.numpy as jnp
from jax import lax
from jax.sharding import PartitionSpec as P

epsilon = 1e-05


def from_behind(x, axis, by):
    size = lax.axis_size(axis)
    pairs = [(i, i + by) for i in range(size) if 0 <= i + by < size]
    return lax.ppermute(x, axis, pairs)


def rms_scale(values):
    return lax.rsqrt(jnp.mean(values * values, axis=-1, keepdims=True) + epsilon)


def attend_block(query, key_part, value_part, carried_low):
    tok_rows = query.shape[0]
    inter = jnp.einsum("thc,hcd->thd", query, carried_low, preferred_element_type=jnp.float32)
    scores = jnp.einsum("thc,shc->hts", query, key_part, preferred_element_type=jnp.float32)
    causal = lax.broadcasted_iota(jnp.int32, (tok_rows, tok_rows), 0) >= lax.broadcasted_iota(
        jnp.int32, (tok_rows, tok_rows), 1
    )
    scores = jnp.where(causal[None], scores, jnp.zeros_like(scores)).astype(jnp.bfloat16)
    intra = jnp.einsum("hts,shd->thd", scores, value_part, preferred_element_type=jnp.float32)
    attn = inter + intra
    return (attn * rms_scale(attn)).astype(jnp.bfloat16)


def attend_blocks(query, key_part, value_part):
    states = jnp.einsum("bthc,bthd->bhcd", key_part, value_part, preferred_element_type=jnp.float32)
    running = jnp.cumsum(states, axis=0)
    carried = jnp.concatenate([jnp.zeros_like(states[:1]), running[:-1]], axis=0)
    return jax.vmap(attend_block)(query, key_part, value_part, carried.astype(jnp.bfloat16))


def project_heads(split, weights):
    mixed = jnp.einsum("thc,hjcd->jthd", split, weights[:, :3], preferred_element_type=jnp.float32)
    return jnp.concatenate([jax.nn.silu(mixed[:2]), mixed[2:]], axis=0).astype(jnp.bfloat16)


def apply_layer(stream, gain, weights):
    tok_rows, width = stream.shape
    head_count, head_size = (weights.shape[0], weights.shape[2])
    wide = stream.astype(jnp.float32)
    normed = (wide * rms_scale(wide) * gain).astype(jnp.bfloat16)
    parts = lax.axis_size("seq")
    group = head_count // parts
    grouped_in = normed.reshape(tok_rows, parts, group * head_size)
    received = lax.all_to_all(grouped_in, "seq", split_axis=1, concat_axis=0, tiled=True)
    owned = lax.dynamic_slice_in_dim(weights, lax.axis_index("seq") * group, group, 0)
    stacked = project_heads(received, owned)
    blocked = stacked.reshape(3, parts, tok_rows, group, head_size)
    local_out = attend_blocks(blocked[0], blocked[1], blocked[2])
    returned = lax.all_to_all(local_out, "seq", split_axis=0, concat_axis=2, tiled=True)
    head_out = returned.reshape(tok_rows, head_count, head_size)
    projected = jnp.einsum(
        "thc,hcd->thd", head_out, weights[:, 3], preferred_element_type=jnp.float32
    )
    return (wide + projected.reshape(tok_rows, width)).astype(jnp.bfloat16)


def on_device(stream_in, norm_gain, proj_weight):
    micro_count, tok_rows, width = stream_in.shape
    section_count = lax.axis_size("section")
    position = lax.axis_index("section")
    gain = norm_gain[0]
    weights = proj_weight[0]
    tick_count = micro_count + section_count - 1

    def one_tick(step_index, carry):
        incoming, saved = carry
        first_input = lax.dynamic_index_in_dim(
            stream_in, jnp.clip(step_index, 0, micro_count - 1).astype(jnp.int32), 0, keepdims=False
        )
        current = jnp.where(position == 0, first_input, incoming)
        result = apply_layer(current, gain, weights)
        slot_index = step_index - position
        valid = jnp.logical_and(slot_index >= 0, slot_index < micro_count)
        target = jnp.clip(slot_index, 0, micro_count - 1)
        previous = lax.dynamic_index_in_dim(saved, target, 0, keepdims=False)
        chosen = jnp.where(valid, result, previous)
        saved = lax.dynamic_update_index_in_dim(saved, chosen, target, 0)
        passed = from_behind(result, "section", 1)
        return (passed, saved)

    initial = (
        jnp.zeros((tok_rows, width), jnp.bfloat16),
        jnp.zeros((micro_count, tok_rows, width), jnp.bfloat16),
    )
    final_carry = lax.fori_loop(0, tick_count, one_tick, initial)
    return final_carry[1][None]


def solution(mesh):
    in_specs = (P(None, "seq", None), P("section", None), P("section", None, None, None, None))
    out_specs = P("section", None, "seq", None)
    return jax.shard_map(
        on_device, mesh=mesh, in_specs=in_specs, out_specs=out_specs, check_vma=False
    )
```

profile of v0, /device:TPU:128, one launch (start us, length us, event | category | flops | bytes accessed | tf_op | source)
XLA Modules:
  0.0 941.7 jit_solution(10498622832662492168)
XLA Ops:
  8.2 933.5 %while.16 = (s32[]{:T(128)}, bf16[128,4096]{0,1:T(8,128)(2,1)S(1)}, bf16[2,128,4096]{2,1,0:T(8,128)(2,1)}, pred[]{:T(512)}, bf16[2,128,4096]{2,1,0:T(8,128)(2,1)...) while((s32[]{:T(128)}, bf16[128,4096]{0,1:T(8,128)(2,1)S(1)}, ...), condition=%wide.region_4.5_spmd, body=%wide.region_0.4_spmd.sunk | while | flops 1105219712 | bytes 95472000 | solution.py:93
  20.2 17.2 %all-to-all-done = bf16[128,32,128]{2,0,1:T(8,128)(2,1)S(1)} async-done(((bf16[128,32,128]{2,0,1:T(8,128)(2,1)}), bf16[128,32,128]{2,0,1:T(8,128)(2,1)S(1)}, u32[]{:S(2)}, u32[]{:S(2)}) %all-to-all-start) | async-done | bytes 1048608 | tf_op jit(solution)/shard_map/while/body/eval_jaxpr/all_to_all | solution.py:52
  91.0 23.9 %collective-permute-done = bf16[128,4096]{0,1:T(8,128)(2,1)S(1)} collective-permute-done((bf16[128,4096]{0,1:T(8,128)(2,1)}, bf16[128,4096]{0,1:T(8,128)(2,1)S(1)}, u32[]{:S(2)}, u32[]{:S(2)}) %collective-permute-start) | collective-permute-done | bytes 1048608 | tf_op jit(solution)/shard_map/while/body/eval_jaxpr/ppermute | solution.py:12
  123.5 17.2 %all-to-all-done = bf16[128,32,128]{2,0,1:T(8,128)(2,1)S(1)} async-done(((bf16[128,32,128]{2,0,1:T(8,128)(2,1)}), bf16[128,32,128]{2,0,1:T(8,128)(2,1)S(1)}, u32[]{:S(2)}, u32[]{:S(2)}) %all-to-all-start) | async-done | bytes 1048608 | tf_op jit(solution)/shard_map/while/body/eval_jaxpr/all_to_all | solution.py:52
  193.3 25.0 %collective-permute-done = bf16[128,4096]{0,1:T(8,128)(2,1)S(1)} collective-permute-done((bf16[128,4096]{0,1:T(8,128)(2,1)}, bf16[128,4096]{0,1:T(8,128)(2,1)S(1)}, u32[]{:S(2)}, u32[]{:S(2)}) %collective-permute-start) | collective-permute-done | bytes 1048608 | tf_op jit(solution)/shard_map/while/body/eval_jaxpr/ppermute | solution.py:12
  226.9 17.2 %all-to-all-done = bf16[128,32,128]{2,0,1:T(8,128)(2,1)S(1)} async-done(((bf16[128,32,128]{2,0,1:T(8,128)(2,1)}), bf16[128,32,128]{2,0,1:T(8,128)(2,1)S(1)}, u32[]{:S(2)}, u32[]{:S(2)}) %all-to-all-start) | async-done | bytes 1048608 | tf_op jit(solution)/shard_map/while/body/eval_jaxpr/all_to_all | solution.py:52
  296.7 25.0 %collective-permute-done = bf16[128,4096]{0,1:T(8,128)(2,1)S(1)} collective-permute-done((bf16[128,4096]{0,1:T(8,128)(2,1)}, bf16[128,4096]{0,1:T(8,128)(2,1)S(1)}, u32[]{:S(2)}, u32[]{:S(2)}) %collective-permute-start) | collective-permute-done | bytes 1048608 | tf_op jit(solution)/shard_map/while/body/eval_jaxpr/ppermute | solution.py:12
  330.2 17.2 %all-to-all-done = bf16[128,32,128]{2,0,1:T(8,128)(2,1)S(1)} async-done(((bf16[128,32,128]{2,0,1:T(8,128)(2,1)}), bf16[128,32,128]{2,0,1:T(8,128)(2,1)S(1)}, u32[]{:S(2)}, u32[]{:S(2)}) %all-to-all-start) | async-done | bytes 1048608 | tf_op jit(solution)/shard_map/while/body/eval_jaxpr/all_to_all | solution.py:52
  378.0 13.3 %all-to-all-done.1 = bf16[32,128,1,128]{1,3,2,0:T(8,128)(2,1)S(1)} async-done(((bf16[32,128,1,128]{1,3,2,0:T(8,128)(2,1)}), bf16[32,128,1,128]{1,3,2,0:T(8,128)(2,1)S(1)}, u32[]{:S(2)}, u32[]{:S(2)}) %all-to-all-start.1) | async-done | bytes 1048608 | tf_op jit(solution)/shard_map/while/body/eval_jaxpr/all_to_all | solution.py:57
  400.0 25.0 %collective-permute-done = bf16[128,4096]{0,1:T(8,128)(2,1)S(1)} collective-permute-done((bf16[128,4096]{0,1:T(8,128)(2,1)}, bf16[128,4096]{0,1:T(8,128)(2,1)S(1)}, u32[]{:S(2)}, u32[]{:S(2)}) %collective-permute-start) | collective-permute-done | bytes 1048608 | tf_op jit(solution)/shard_map/while/body/eval_jaxpr/ppermute | solution.py:12
  433.6 17.2 %all-to-all-done = bf16[128,32,128]{2,0,1:T(8,128)(2,1)S(1)} async-done(((bf16[128,32,128]{2,0,1:T(8,128)(2,1)}), bf16[128,32,128]{2,0,1:T(8,128)(2,1)S(1)}, u32[]{:S(2)}, u32[]{:S(2)}) %all-to-all-start) | async-done | bytes 1048608 | tf_op jit(solution)/shard_map/while/body/eval_jaxpr/all_to_all | solution.py:52
  481.4 13.3 %all-to-all-done.1 = bf16[32,128,1,128]{1,3,2,0:T(8,128)(2,1)S(1)} async-done(((bf16[32,128,1,128]{1,3,2,0:T(8,128)(2,1)}), bf16[32,128,1,128]{1,3,2,0:T(8,128)(2,1)S(1)}, u32[]{:S(2)}, u32[]{:S(2)}) %all-to-all-start.1) | async-done | bytes 1048608 | tf_op jit(solution)/shard_map/while/body/eval_jaxpr/all_to_all | solution.py:57
  503.4 25.0 %collective-permute-done = bf16[128,4096]{0,1:T(8,128)(2,1)S(1)} collective-permute-done((bf16[128,4096]{0,1:T(8,128)(2,1)}, bf16[128,4096]{0,1:T(8,128)(2,1)S(1)}, u32[]{:S(2)}, u32[]{:S(2)}) %collective-permute-start) | collective-permute-done | bytes 1048608 | tf_op jit(solution)/shard_map/while/body/eval_jaxpr/ppermute | solution.py:12
  536.9 17.2 %all-to-all-done = bf16[128,32,128]{2,0,1:T(8,128)(2,1)S(1)} async-done(((bf16[128,32,128]{2,0,1:T(8,128)(2,1)}), bf16[128,32,128]{2,0,1:T(8,128)(2,1)S(1)}, u32[]{:S(2)}, u32[]{:S(2)}) %all-to-all-start) | async-done | bytes 1048608 | tf_op jit(solution)/shard_map/while/body/eval_jaxpr/all_to_all | solution.py:52
  584.7 13.3 %all-to-all-done.1 = bf16[32,128,1,128]{1,3,2,0:T(8,128)(2,1)S(1)} async-done(((bf16[32,128,1,128]{1,3,2,0:T(8,128)(2,1)}), bf16[32,128,1,128]{1,3,2,0:T(8,128)(2,1)S(1)}, u32[]{:S(2)}, u32[]{:S(2)}) %all-to-all-start.1) | async-done | bytes 1048608 | tf_op jit(solution)/shard_map/while/body/eval_jaxpr/all_to_all | solution.py:57
  606.7 25.0 %collective-permute-done = bf16[128,4096]{0,1:T(8,128)(2,1)S(1)} collective-permute-done((bf16[128,4096]{0,1:T(8,128)(2,1)}, bf16[128,4096]{0,1:T(8,128)(2,1)S(1)}, u32[]{:S(2)}, u32[]{:S(2)}) %collective-permute-start) | collective-permute-done | bytes 1048608 | tf_op jit(solution)/shard_map/while/body/eval_jaxpr/ppermute | solution.py:12
  640.2 17.2 %all-to-all-done = bf16[128,32,128]{2,0,1:T(8,128)(2,1)S(1)} async-done(((bf16[128,32,128]{2,0,1:T(8,128)(2,1)}), bf16[128,32,128]{2,0,1:T(8,128)(2,1)S(1)}, u32[]{:S(2)}, u32[]{:S(2)}) %all-to-all-start) | async-done | bytes 1048608 | tf_op jit(solution)/shard_map/while/body/eval_jaxpr/all_to_all | solution.py:52
  688.1 13.3 %all-to-all-done.1 = bf16[32,128,1,128]{1,3,2,0:T(8,128)(2,1)S(1)} async-done(((bf16[32,128,1,128]{1,3,2,0:T(8,128)(2,1)}), bf16[32,128,1,128]{1,3,2,0:T(8,128)(2,1)S(1)}, u32[]{:S(2)}, u32[]{:S(2)}) %all-to-all-start.1) | async-done | bytes 1048608 | tf_op jit(solution)/shard_map/while/body/eval_jaxpr/all_to_all | solution.py:57
  710.0 25.0 %collective-permute-done = bf16[128,4096]{0,1:T(8,128)(2,1)S(1)} collective-permute-done((bf16[128,4096]{0,1:T(8,128)(2,1)}, bf16[128,4096]{0,1:T(8,128)(2,1)S(1)}, u32[]{:S(2)}, u32[]{:S(2)}) %collective-permute-start) | collective-permute-done | bytes 1048608 | tf_op jit(solution)/shard_map/while/body/eval_jaxpr/ppermute | solution.py:12
  743.6 17.2 %all-to-all-done = bf16[128,32,128]{2,0,1:T(8,128)(2,1)S(1)} async-done(((bf16[128,32,128]{2,0,1:T(8,128)(2,1)}), bf16[128,32,128]{2,0,1:T(8,128)(2,1)S(1)}, u32[]{:S(2)}, u32[]{:S(2)}) %all-to-all-start) | async-done | bytes 1048608 | tf_op jit(solution)/shard_map/while/body/eval_jaxpr/all_to_all | solution.py:52
  791.4 13.3 %all-to-all-done.1 = bf16[32,128,1,128]{1,3,2,0:T(8,128)(2,1)S(1)} async-done(((bf16[32,128,1,128]{1,3,2,0:T(8,128)(2,1)}), bf16[32,128,1,128]{1,3,2,0:T(8,128)(2,1)S(1)}, u32[]{:S(2)}, u32[]{:S(2)}) %all-to-all-start.1) | async-done | bytes 1048608 | tf_op jit(solution)/shard_map/while/body/eval_jaxpr/all_to_all | solution.py:57
  813.4 25.0 %collective-permute-done = bf16[128,4096]{0,1:T(8,128)(2,1)S(1)} collective-permute-done((bf16[128,4096]{0,1:T(8,128)(2,1)}, bf16[128,4096]{0,1:T(8,128)(2,1)S(1)}, u32[]{:S(2)}, u32[]{:S(2)}) %collective-permute-start) | collective-permute-done | bytes 1048608 | tf_op jit(solution)/shard_map/while/body/eval_jaxpr/ppermute | solution.py:12
  846.9 17.2 %all-to-all-done = bf16[128,32,128]{2,0,1:T(8,128)(2,1)S(1)} async-done(((bf16[128,32,128]{2,0,1:T(8,128)(2,1)}), bf16[128,32,128]{2,0,1:T(8,128)(2,1)S(1)}, u32[]{:S(2)}, u32[]{:S(2)}) %all-to-all-start) | async-done | bytes 1048608 | tf_op jit(solution)/shard_map/while/body/eval_jaxpr/all_to_all | solution.py:52
  916.7 25.0 %collective-permute-done = bf16[128,4096]{0,1:T(8,128)(2,1)S(1)} collective-permute-done((bf16[128,4096]{0,1:T(8,128)(2,1)}, bf16[128,4096]{0,1:T(8,128)(2,1)S(1)}, u32[]{:S(2)}, u32[]{:S(2)}) %collective-permute-start) | collective-permute-done | bytes 1048608 | tf_op jit(solution)/shard_map/while/body/eval_jaxpr/ppermute | solution.py:12
  (297 shorter events, 495.8 us)
Async XLA Ops:
  12.8 24.5 %all-to-all-start = ((bf16[128,32,128]{2,0,1:T(8,128)(2,1)}), bf16[128,32,128]{2,0,1:T(8,128)(2,1)S(1)}, u32[]{:S(2)}, u32[]{:S(2)}) async-start(bf16[128,32,128]{2,0,1:T(8,128)(2,1)} %copy.74), calls=%async_computation | async-start | bytes 2097152 | tf_op jit(solution)/shard_map/while/body/eval_jaxpr/all_to_all | solution.py:52
  60.1 21.1 %all-to-all-start.1 = ((bf16[32,128,1,128]{1,3,2,0:T(8,128)(2,1)}), bf16[32,128,1,128]{1,3,2,0:T(8,128)(2,1)S(1)}, u32[]{:S(2)}, u32[]{:S(2)}) async-start(bf16[32,128,1,128]{1,3,2,0:T(8,128)(2,1)} %fusion.71), calls=%async_computation.1 | async-start | bytes 2097152 | tf_op jit(solution)/shard_map/while/body/eval_jaxpr/all_to_all | solution.py:57
  86.5 28.5 %collective-permute-start = (bf16[128,4096]{0,1:T(8,128)(2,1)}, bf16[128,4096]{0,1:T(8,128)(2,1)S(1)}, u32[]{:S(2)}, u32[]{:S(2)}) collective-permute-start(bf16[128,4096]{0,1:T(8,128)(2,1)} %get-tuple-element.266), channel_id=1, source_target_pairs={{0,32},{32,64},{64,96},{96,128},{128,160},{160,192},{192,224},{1,3... | collective-permute-start | bytes 3145736 | tf_op jit(solution)/shard_map/while/body/eval_jaxpr/ppermute | solution.py:12
  119.6 21.1 %all-to-all-start = ((bf16[128,32,128]{2,0,1:T(8,128)(2,1)}), bf16[128,32,128]{2,0,1:T(8,128)(2,1)S(1)}, u32[]{:S(2)}, u32[]{:S(2)}) async-start(bf16[128,32,128]{2,0,1:T(8,128)(2,1)} %copy.74), calls=%async_computation | async-start | bytes 2097152 | tf_op jit(solution)/shard_map/while/body/eval_jaxpr/all_to_all | solution.py:52
  163.5 21.1 %all-to-all-start.1 = ((bf16[32,128,1,128]{1,3,2,0:T(8,128)(2,1)}), bf16[32,128,1,128]{1,3,2,0:T(8,128)(2,1)S(1)}, u32[]{:S(2)}, u32[]{:S(2)}) async-start(bf16[32,128,1,128]{1,3,2,0:T(8,128)(2,1)} %fusion.71), calls=%async_computation.1 | async-start | bytes 2097152 | tf_op jit(solution)/shard_map/while/body/eval_jaxpr/all_to_all | solution.py:57
  189.8 28.5 %collective-permute-start = (bf16[128,4096]{0,1:T(8,128)(2,1)}, bf16[128,4096]{0,1:T(8,128)(2,1)S(1)}, u32[]{:S(2)}, u32[]{:S(2)}) collective-permute-start(bf16[128,4096]{0,1:T(8,128)(2,1)} %get-tuple-element.266), channel_id=1, source_target_pairs={{0,32},{32,64},{64,96},{96,128},{128,160},{160,192},{192,224},{1,3... | collective-permute-start | bytes 3145736 | tf_op jit(solution)/shard_map/while/body/eval_jaxpr/ppermute | solution.py:12
  222.9 21.1 %all-to-all-start = ((bf16[128,32,128]{2,0,1:T(8,128)(2,1)}), bf16[128,32,128]{2,0,1:T(8,128)(2,1)S(1)}, u32[]{:S(2)}, u32[]{:S(2)}) async-start(bf16[128,32,128]{2,0,1:T(8,128)(2,1)} %copy.74), calls=%async_computation | async-start | bytes 2097152 | tf_op jit(solution)/shard_map/while/body/eval_jaxpr/all_to_all | solution.py:52
  266.8 21.1 %all-to-all-start.1 = ((bf16[32,128,1,128]{1,3,2,0:T(8,128)(2,1)}), bf16[32,128,1,128]{1,3,2,0:T(8,128)(2,1)S(1)}, u32[]{:S(2)}, u32[]{:S(2)}) async-start(bf16[32,128,1,128]{1,3,2,0:T(8,128)(2,1)} %fusion.71), calls=%async_computation.1 | async-start | bytes 2097152 | tf_op jit(solution)/shard_map/while/body/eval_jaxpr/all_to_all | solution.py:57
  293.2 28.5 %collective-permute-start = (bf16[128,4096]{0,1:T(8,128)(2,1)}, bf16[128,4096]{0,1:T(8,128)(2,1)S(1)}, u32[]{:S(2)}, u32[]{:S(2)}) collective-permute-start(bf16[128,4096]{0,1:T(8,128)(2,1)} %get-tuple-element.266), channel_id=1, source_target_pairs={{0,32},{32,64},{64,96},{96,128},{128,160},{160,192},{192,224},{1,3... | collective-permute-start | bytes 3145736 | tf_op jit(solution)/shard_map/while/body/eval_jaxpr/ppermute | solution.py:12
  326.2 21.1 %all-to-all-start = ((bf16[128,32,128]{2,0,1:T(8,128)(2,1)}), bf16[128,32,128]{2,0,1:T(8,128)(2,1)S(1)}, u32[]{:S(2)}, u32[]{:S(2)}) async-start(bf16[128,32,128]{2,0,1:T(8,128)(2,1)} %copy.74), calls=%async_computation | async-start | bytes 2097152 | tf_op jit(solution)/shard_map/while/body/eval_jaxpr/all_to_all | solution.py:52
  370.2 21.1 %all-to-all-start.1 = ((bf16[32,128,1,128]{1,3,2,0:T(8,128)(2,1)}), bf16[32,128,1,128]{1,3,2,0:T(8,128)(2,1)S(1)}, u32[]{:S(2)}, u32[]{:S(2)}) async-start(bf16[32,128,1,128]{1,3,2,0:T(8,128)(2,1)} %fusion.71), calls=%async_computation.1 | async-start | bytes 2097152 | tf_op jit(solution)/shard_map/while/body/eval_jaxpr/all_to_all | solution.py:57
  396.5 28.5 %collective-permute-start = (bf16[128,4096]{0,1:T(8,128)(2,1)}, bf16[128,4096]{0,1:T(8,128)(2,1)S(1)}, u32[]{:S(2)}, u32[]{:S(2)}) collective-permute-start(bf16[128,4096]{0,1:T(8,128)(2,1)} %get-tuple-element.266), channel_id=1, source_target_pairs={{0,32},{32,64},{64,96},{96,128},{128,160},{160,192},{192,224},{1,3... | collective-permute-start | bytes 3145736 | tf_op jit(solution)/shard_map/while/body/eval_jaxpr/ppermute | solution.py:12
  429.6 21.1 %all-to-all-start = ((bf16[128,32,128]{2,0,1:T(8,128)(2,1)}), bf16[128,32,128]{2,0,1:T(8,128)(2,1)S(1)}, u32[]{:S(2)}, u32[]{:S(2)}) async-start(bf16[128,32,128]{2,0,1:T(8,128)(2,1)} %copy.74), calls=%async_computation | async-start | bytes 2097152 | tf_op jit(solution)/shard_map/while/body/eval_jaxpr/all_to_all | solution.py:52
  473.5 21.1 %all-to-all-start.1 = ((bf16[32,128,1,128]{1,3,2,0:T(8,128)(2,1)}), bf16[32,128,1,128]{1,3,2,0:T(8,128)(2,1)S(1)}, u32[]{:S(2)}, u32[]{:S(2)}) async-start(bf16[32,128,1,128]{1,3,2,0:T(8,128)(2,1)} %fusion.71), calls=%async_computation.1 | async-start | bytes 2097152 | tf_op jit(solution)/shard_map/while/body/eval_jaxpr/all_to_all | solution.py:57
  499.8 28.5 %collective-permute-start = (bf16[128,4096]{0,1:T(8,128)(2,1)}, bf16[128,4096]{0,1:T(8,128)(2,1)S(1)}, u32[]{:S(2)}, u32[]{:S(2)}) collective-permute-start(bf16[128,4096]{0,1:T(8,128)(2,1)} %get-tuple-element.266), channel_id=1, source_target_pairs={{0,32},{32,64},{64,96},{96,128},{128,160},{160,192},{192,224},{1,3... | collective-permute-start | bytes 3145736 | tf_op jit(solution)/shard_map/while/body/eval_jaxpr/ppermute | solution.py:12
  532.9 21.1 %all-to-all-start = ((bf16[128,32,128]{2,0,1:T(8,128)(2,1)}), bf16[128,32,128]{2,0,1:T(8,128)(2,1)S(1)}, u32[]{:S(2)}, u32[]{:S(2)}) async-start(bf16[128,32,128]{2,0,1:T(8,128)(2,1)} %copy.74), calls=%async_computation | async-start | bytes 2097152 | tf_op jit(solution)/shard_map/while/body/eval_jaxpr/all_to_all | solution.py:52
  576.9 21.1 %all-to-all-start.1 = ((bf16[32,128,1,128]{1,3,2,0:T(8,128)(2,1)}), bf16[32,128,1,128]{1,3,2,0:T(8,128)(2,1)S(1)}, u32[]{:S(2)}, u32[]{:S(2)}) async-start(bf16[32,128,1,128]{1,3,2,0:T(8,128)(2,1)} %fusion.71), calls=%async_computation.1 | async-start | bytes 2097152 | tf_op jit(solution)/shard_map/while/body/eval_jaxpr/all_to_all | solution.py:57
  603.2 28.5 %collective-permute-start = (bf16[128,4096]{0,1:T(8,128)(2,1)}, bf16[128,4096]{0,1:T(8,128)(2,1)S(1)}, u32[]{:S(2)}, u32[]{:S(2)}) collective-permute-start(bf16[128,4096]{0,1:T(8,128)(2,1)} %get-tuple-element.266), channel_id=1, source_target_pairs={{0,32},{32,64},{64,96},{96,128},{128,160},{160,192},{192,224},{1,3... | collective-permute-start | bytes 3145736 | tf_op jit(solution)/shard_map/while/body/eval_jaxpr/ppermute | solution.py:12
  636.3 21.1 %all-to-all-start = ((bf16[128,32,128]{2,0,1:T(8,128)(2,1)}), bf16[128,32,128]{2,0,1:T(8,128)(2,1)S(1)}, u32[]{:S(2)}, u32[]{:S(2)}) async-start(bf16[128,32,128]{2,0,1:T(8,128)(2,1)} %copy.74), calls=%async_computation | async-start | bytes 2097152 | tf_op jit(solution)/shard_map/while/body/eval_jaxpr/all_to_all | solution.py:52
  706.5 28.5 %collective-permute-start = (bf16[128,4096]{0,1:T(8,128)(2,1)}, bf16[128,4096]{0,1:T(8,128)(2,1)S(1)}, u32[]{:S(2)}, u32[]{:S(2)}) collective-permute-start(bf16[128,4096]{0,1:T(8,128)(2,1)} %get-tuple-element.266), channel_id=1, source_target_pairs={{0,32},{32,64},{64,96},{96,128},{128,160},{160,192},{192,224},{1,3... | collective-permute-start | bytes 3145736 | tf_op jit(solution)/shard_map/while/body/eval_jaxpr/ppermute | solution.py:12
  739.6 21.1 %all-to-all-start = ((bf16[128,32,128]{2,0,1:T(8,128)(2,1)}), bf16[128,32,128]{2,0,1:T(8,128)(2,1)S(1)}, u32[]{:S(2)}, u32[]{:S(2)}) async-start(bf16[128,32,128]{2,0,1:T(8,128)(2,1)} %copy.74), calls=%async_computation | async-start | bytes 2097152 | tf_op jit(solution)/shard_map/while/body/eval_jaxpr/all_to_all | solution.py:52
  809.9 28.5 %collective-permute-start = (bf16[128,4096]{0,1:T(8,128)(2,1)}, bf16[128,4096]{0,1:T(8,128)(2,1)S(1)}, u32[]{:S(2)}, u32[]{:S(2)}) collective-permute-start(bf16[128,4096]{0,1:T(8,128)(2,1)} %get-tuple-element.266), channel_id=1, source_target_pairs={{0,32},{32,64},{64,96},{96,128},{128,160},{160,192},{192,224},{1,3... | collective-permute-start | bytes 3145736 | tf_op jit(solution)/shard_map/while/body/eval_jaxpr/ppermute | solution.py:12
  843.0 21.1 %all-to-all-start = ((bf16[128,32,128]{2,0,1:T(8,128)(2,1)}), bf16[128,32,128]{2,0,1:T(8,128)(2,1)S(1)}, u32[]{:S(2)}, u32[]{:S(2)}) async-start(bf16[128,32,128]{2,0,1:T(8,128)(2,1)} %copy.74), calls=%async_computation | async-start | bytes 2097152 | tf_op jit(solution)/shard_map/while/body/eval_jaxpr/all_to_all | solution.py:52
  913.2 28.5 %collective-permute-start = (bf16[128,4096]{0,1:T(8,128)(2,1)}, bf16[128,4096]{0,1:T(8,128)(2,1)S(1)}, u32[]{:S(2)}, u32[]{:S(2)}) collective-permute-start(bf16[128,4096]{0,1:T(8,128)(2,1)} %get-tuple-element.266), channel_id=1, source_target_pairs={{0,32},{32,64},{64,96},{96,128},{128,160},{160,192},{192,224},{1,3... | collective-permute-start | bytes 3145736 | tf_op jit(solution)/shard_map/while/body/eval_jaxpr/ppermute | solution.py:12
  (4 other events, 65.1 us)
where the time goes:
time: 947 us; the launch traced here: 942 us
  waiting for transfers between devices  498 us (53%)
  local copies, waits for them, and re-layouts  167 us (18%)
  matrix products  121 us (13%)
  starting transfers between devices  92.3 us (10%)
  other arithmetic  62.3 us (7%)
    ppermute x9, waiting for transfers between devices, from_behind(): return lax.ppermute(x, axis, pairs)  224 us
    all_to_all x9, waiting for transfers between devices, apply_layer(): lax.all_to_all(grouped_in, 'seq', split_axis=1, concat_axis=0, tiled=True)  155 us
    all_to_all x9, waiting for transfers between devices, apply_layer(): lax.all_to_all(local_out, 'seq', split_axis=0, concat_axis=2, tiled=True)  119 us
    dot_general x9, matrix products, attend_block(): jnp.einsum('hts,shd->thd', scores, value_part, preferred_element_type=jnp...  42.9 us
    all_to_all x9, starting transfers between devices, apply_layer(): lax.all_to_all(grouped_in, 'seq', split_axis=1, concat_axis=0, tiled=True)  38.8 us
    while x45, local copies, waits for them, and re-layouts  36.7 us
    all_to_all x9, starting transfers between devices, apply_layer(): lax.all_to_all(local_out, 'seq', split_axis=0, concat_axis=2, tiled=True)  35.3 us
    dynamic_slice x18, local copies, waits for them, and re-layouts, one_tick(): previous = lax.dynamic_index_in_dim(saved, target, 0, keepdims=False)  35.2 us
  transfers between devices with their start and end apart: 27, of which 27 were waited for; matrix products, arithmetic and copies ran while one was open for 5% of the time, Pallas kernels for 0%

commit v1 on v0

--- a/solution.py
+++ b/solution.py
@@ -54,7 +54,10 @@
     stacked = project_heads(received, owned)
     blocked = stacked.reshape(3, parts, tok_rows, group, head_size)
     local_out = attend_blocks(blocked[0], blocked[1], blocked[2])
-    returned = lax.all_to_all(local_out, "seq", split_axis=0, concat_axis=2, tiled=True)
+    count = lax.axis_size("seq")
+    blocks = jnp.stack(jnp.split(local_out, count, axis=0), axis=0)
+    blocks = lax.all_to_all(blocks, "seq", split_axis=0, concat_axis=0)
+    returned = jnp.concatenate(blocks, axis=2)
     head_out = returned.reshape(tok_rows, head_count, head_size)
     projected = jnp.einsum(
         "thc,hcd->thd", head_out, weights[:, 3], preferred_element_type=jnp.float32

time: 947 us -> 1100 us (1.16)
  local copies, waits for them, and re-layouts: 167 us -> 311 us
  waiting for transfers between devices: 498 us -> 515 us
    while x45 -> x324, local copies, waits for them, and re-layouts: 36.7 us -> 205 us
    dynamic_slice x18, local copies, waits for them, and re-layouts: 35.2 us -> 17.6 us  [one_tick(): previous = lax.dynamic_index_in_dim(saved, target, 0, keepdims=False)]
    all_to_all x9, waiting for transfers between devices: 119 us -> 137 us  [apply_layer(): blocks = lax.all_to_all(blocks, 'seq', split_axis=0, concat_axis=0)]
    all_to_all x9 -> x0, local copies, waits for them, and re-layouts: 12 us -> none  [apply_layer(): lax.all_to_all(local_out, 'seq', split_axis=0, concat_axis=2, tiled=True)]
    another operation x9 -> x18, local copies, waits for them, and re-layouts: 20.4 us -> 25.9 us
  transfers between devices with their start and end apart: 27 -> 27, of which waited for: 27 -> 27; matrix products, arithmetic and copies ran while one was open for 5% -> 3% of each run, Pallas kernels for 0% -> 0%
where the time goes in v1:
time: 1100 us
  waiting for transfers between devices  515 us (47%)
  local copies, waits for them, and re-layouts  311 us (28%)
  matrix products  117 us (11%)
  starting transfers between devices  98.9 us (9%)
  other arithmetic  55.3 us (5%)
    ppermute x9, waiting for transfers between devices, from_behind(): return lax.ppermute(x, axis, pairs)  224 us
    while x324, local copies, waits for them, and re-layouts  205 us
    all_to_all x9, waiting for transfers between devices, apply_layer(): lax.all_to_all(grouped_in, 'seq', split_axis=1, concat_axis=0, tiled=True)  155 us
    all_to_all x9, waiting for transfers between devices, apply_layer(): blocks = lax.all_to_all(blocks, 'seq', split_axis=0, concat_axis=0)  137 us
    dot_general x9, matrix products, attend_block(): jnp.einsum('hts,shd->thd', scores, value_part, preferred_element_type=jnp...  42.9 us
    all_to_all x9, starting transfers between devices, apply_layer(): blocks = lax.all_to_all(blocks, 'seq', split_axis=0, concat_axis=0)  41.9 us
    all_to_all x9, starting transfers between devices, apply_layer(): lax.all_to_all(grouped_in, 'seq', split_axis=1, concat_axis=0, tiled=True)  38.8 us
    dot_general x9, matrix products, attend_block(): jnp.einsum('thc,hcd->thd', query, carried_low, preferred_element_type=jnp...  33.1 us
  transfers between devices with their start and end apart: 27, of which 27 were waited for; matrix products, arithmetic and copies ran while one was open for 3% of the time, Pallas kernels for 0%

profile of v1, /device:TPU:128, one launch (start us, length us, event | category | flops | bytes accessed | tf_op | source)
XLA Modules:
  0.0 1099.2 jit_solution(2733746130287784773)
XLA Ops:
  8.2 1091.1 %while.16 = (s32[]{:T(128)}, bf16[128,4096]{0,1:T(8,128)(2,1)S(1)}, bf16[2,128,4096]{2,1,0:T(8,128)(2,1)}, pred[]{:T(512)}, bf16[2,128,4096]{2,1,0:T(8,128)(2,1)...) while((s32[]{:T(128)}, bf16[128,4096]{0,1:T(8,128)(2,1)S(1)}, ...), condition=%wide.region_4.5_spmd, body=%wide.region_0.4_spmd.sunk | while | flops 1105219712 | bytes 96520576 | solution.py:96
  20.1 17.2 %all-to-all-done = bf16[128,32,128]{2,0,1:T(8,128)(2,1)S(1)} async-done(((bf16[128,32,128]{2,0,1:T(8,128)(2,1)}), bf16[128,32,128]{2,0,1:T(8,128)(2,1)S(1)}, u32[]{:S(2)}, u32[]{:S(2)}) %all-to-all-start) | async-done | bytes 1048608 | tf_op jit(solution)/shard_map/while/body/eval_jaxpr/all_to_all | solution.py:52
  85.3 15.2 %all-to-all-done.1 = bf16[32,1,128,1,128]{2,4,3,1,0:T(8,128)(2,1)} async-done(((bf16[32,1,128,1,128]{2,4,3,1,0:T(8,128)(2,1)}), bf16[32,1,128,1,128]{2,4,3,1,0:T(8,128)(2,1)}, u32[]{:S(2)}, u32[]{:S(2)}) %all-to-all-start.1) | async-done | bytes 1048608 | tf_op jit(solution)/shard_map/while/body/eval_jaxpr/all_to_all | solution.py:59
  108.5 24.0 %collective-permute-done = bf16[128,4096]{0,1:T(8,128)(2,1)S(1)} collective-permute-done((bf16[128,4096]{0,1:T(8,128)(2,1)}, bf16[128,4096]{0,1:T(8,128)(2,1)S(1)}, u32[]{:S(2)}, u32[]{:S(2)}) %collective-permute-start) | collective-permute-done | bytes 1048608 | tf_op jit(solution)/shard_map/while/body/eval_jaxpr/ppermute | solution.py:12
  141.0 17.2 %all-to-all-done = bf16[128,32,128]{2,0,1:T(8,128)(2,1)S(1)} async-done(((bf16[128,32,128]{2,0,1:T(8,128)(2,1)}), bf16[128,32,128]{2,0,1:T(8,128)(2,1)S(1)}, u32[]{:S(2)}, u32[]{:S(2)}) %all-to-all-start) | async-done | bytes 1048608 | tf_op jit(solution)/shard_map/while/body/eval_jaxpr/all_to_all | solution.py:52
  228.3 25.0 %collective-permute-done = bf16[128,4096]{0,1:T(8,128)(2,1)S(1)} collective-permute-done((bf16[128,4096]{0,1:T(8,128)(2,1)}, bf16[128,4096]{0,1:T(8,128)(2,1)S(1)}, u32[]{:S(2)}, u32[]{:S(2)}) %collective-permute-start) | collective-permute-done | bytes 1048608 | tf_op jit(solution)/shard_map/while/body/eval_jaxpr/ppermute | solution.py:12
  261.8 17.2 %all-to-all-done = bf16[128,32,128]{2,0,1:T(8,128)(2,1)S(1)} async-done(((bf16[128,32,128]{2,0,1:T(8,128)(2,1)}), bf16[128,32,128]{2,0,1:T(8,128)(2,1)S(1)}, u32[]{:S(2)}, u32[]{:S(2)}) %all-to-all-start) | async-done | bytes 1048608 | tf_op jit(solution)/shard_map/while/body/eval_jaxpr/all_to_all | solution.py:52
  327.0 15.2 %all-to-all-done.1 = bf16[32,1,128,1,128]{2,4,3,1,0:T(8,128)(2,1)} async-done(((bf16[32,1,128,1,128]{2,4,3,1,0:T(8,128)(2,1)}), bf16[32,1,128,1,128]{2,4,3,1,0:T(8,128)(2,1)}, u32[]{:S(2)}, u32[]{:S(2)}) %all-to-all-start.1) | async-done | bytes 1048608 | tf_op jit(solution)/shard_map/while/body/eval_jaxpr/all_to_all | solution.py:59
  349.1 25.0 %collective-permute-done = bf16[128,4096]{0,1:T(8,128)(2,1)S(1)} collective-permute-done((bf16[128,4096]{0,1:T(8,128)(2,1)}, bf16[128,4096]{0,1:T(8,128)(2,1)S(1)}, u32[]{:S(2)}, u32[]{:S(2)}) %collective-permute-start) | collective-permute-done | bytes 1048608 | tf_op jit(solution)/shard_map/while/body/eval_jaxpr/ppermute | solution.py:12
  382.7 17.2 %all-to-all-done = bf16[128,32,128]{2,0,1:T(8,128)(2,1)S(1)} async-done(((bf16[128,32,128]{2,0,1:T(8,128)(2,1)}), bf16[128,32,128]{2,0,1:T(8,128)(2,1)S(1)}, u32[]{:S(2)}, u32[]{:S(2)}) %all-to-all-start) | async-done | bytes 1048608 | tf_op jit(solution)/shard_map/while/body/eval_jaxpr/all_to_all | solution.py:52
  447.9 15.2 %all-to-all-done.1 = bf16[32,1,128,1,128]{2,4,3,1,0:T(8,128)(2,1)} async-done(((bf16[32,1,128,1,128]{2,4,3,1,0:T(8,128)(2,1)}), bf16[32,1,128,1,128]{2,4,3,1,0:T(8,128)(2,1)}, u32[]{:S(2)}, u32[]{:S(2)}) %all-to-all-start.1) | async-done | bytes 1048608 | tf_op jit(solution)/shard_map/while/body/eval_jaxpr/all_to_all | solution.py:59
  470.0 25.0 %collective-permute-done = bf16[128,4096]{0,1:T(8,128)(2,1)S(1)} collective-permute-done((bf16[128,4096]{0,1:T(8,128)(2,1)}, bf16[128,4096]{0,1:T(8,128)(2,1)S(1)}, u32[]{:S(2)}, u32[]{:S(2)}) %collective-permute-start) | collective-permute-done | bytes 1048608 | tf_op jit(solution)/shard_map/while/body/eval_jaxpr/ppermute | solution.py:12
  503.5 17.2 %all-to-all-done = bf16[128,32,128]{2,0,1:T(8,128)(2,1)S(1)} async-done(((bf16[128,32,128]{2,0,1:T(8,128)(2,1)}), bf16[128,32,128]{2,0,1:T(8,128)(2,1)S(1)}, u32[]{:S(2)}, u32[]{:S(2)}) %all-to-all-start) | async-done | bytes 1048608 | tf_op jit(solution)/shard_map/while/body/eval_jaxpr/all_to_all | solution.py:52
  568.7 15.2 %all-to-all-done.1 = bf16[32,1,128,1,128]{2,4,3,1,0:T(8,128)(2,1)} async-done(((bf16[32,1,128,1,128]{2,4,3,1,0:T(8,128)(2,1)}), bf16[32,1,128,1,128]{2,4,3,1,0:T(8,128)(2,1)}, u32[]{:S(2)}, u32[]{:S(2)}) %all-to-all-start.1) | async-done | bytes 1048608 | tf_op jit(solution)/shard_map/while/body/eval_jaxpr/all_to_all | solution.py:59
  590.8 25.0 %collective-permute-done = bf16[128,4096]{0,1:T(8,128)(2,1)S(1)} collective-permute-done((bf16[128,4096]{0,1:T(8,128)(2,1)}, bf16[128,4096]{0,1:T(8,128)(2,1)S(1)}, u32[]{:S(2)}, u32[]{:S(2)}) %collective-permute-start) | collective-permute-done | bytes 1048608 | tf_op jit(solution)/shard_map/while/body/eval_jaxpr/ppermute | solution.py:12
  624.4 17.2 %all-to-all-done = bf16[128,32,128]{2,0,1:T(8,128)(2,1)S(1)} async-done(((bf16[128,32,128]{2,0,1:T(8,128)(2,1)}), bf16[128,32,128]{2,0,1:T(8,128)(2,1)S(1)}, u32[]{:S(2)}, u32[]{:S(2)}) %all-to-all-start) | async-done | bytes 1048608 | tf_op jit(solution)/shard_map/while/body/eval_jaxpr/all_to_all | solution.py:52
  689.6 15.2 %all-to-all-done.1 = bf16[32,1,128,1,128]{2,4,3,1,0:T(8,128)(2,1)} async-done(((bf16[32,1,128,1,128]{2,4,3,1,0:T(8,128)(2,1)}), bf16[32,1,128,1,128]{2,4,3,1,0:T(8,128)(2,1)}, u32[]{:S(2)}, u32[]{:S(2)}) %all-to-all-start.1) | async-done | bytes 1048608 | tf_op jit(solution)/shard_map/while/body/eval_jaxpr/all_to_all | solution.py:59
  711.7 25.0 %collective-permute-done = bf16[128,4096]{0,1:T(8,128)(2,1)S(1)} collective-permute-done((bf16[128,4096]{0,1:T(8,128)(2,1)}, bf16[128,4096]{0,1:T(8,128)(2,1)S(1)}, u32[]{:S(2)}, u32[]{:S(2)}) %collective-permute-start) | collective-permute-done | bytes 1048608 | tf_op jit(solution)/shard_map/while/body/eval_jaxpr/ppermute | solution.py:12
  745.2 17.2 %all-to-all-done = bf16[128,32,128]{2,0,1:T(8,128)(2,1)S(1)} async-done(((bf16[128,32,128]{2,0,1:T(8,128)(2,1)}), bf16[128,32,128]{2,0,1:T(8,128)(2,1)S(1)}, u32[]{:S(2)}, u32[]{:S(2)}) %all-to-all-start) | async-done | bytes 1048608 | tf_op jit(solution)/shard_map/while/body/eval_jaxpr/all_to_all | solution.py:52
  832.5 25.0 %collective-permute-done = bf16[128,4096]{0,1:T(8,128)(2,1)S(1)} collective-permute-done((bf16[128,4096]{0,1:T(8,128)(2,1)}, bf16[128,4096]{0,1:T(8,128)(2,1)S(1)}, u32[]{:S(2)}, u32[]{:S(2)}) %collective-permute-start) | collective-permute-done | bytes 1048608 | tf_op jit(solution)/shard_map/while/body/eval_jaxpr/ppermute | solution.py:12
  866.1 17.2 %all-to-all-done = bf16[128,32,128]{2,0,1:T(8,128)(2,1)S(1)} async-done(((bf16[128,32,128]{2,0,1:T(8,128)(2,1)}), bf16[128,32,128]{2,0,1:T(8,128)(2,1)S(1)}, u32[]{:S(2)}, u32[]{:S(2)}) %all-to-all-start) | async-done | bytes 1048608 | tf_op jit(solution)/shard_map/while/body/eval_jaxpr/all_to_all | solution.py:52
  953.4 25.0 %collective-permute-done = bf16[128,4096]{0,1:T(8,128)(2,1)S(1)} collective-permute-done((bf16[128,4096]{0,1:T(8,128)(2,1)}, bf16[128,4096]{0,1:T(8,128)(2,1)S(1)}, u32[]{:S(2)}, u32[]{:S(2)}) %collective-permute-start) | collective-permute-done | bytes 1048608 | tf_op jit(solution)/shard_map/while/body/eval_jaxpr/ppermute | solution.py:12
  986.9 17.2 %all-to-all-done = bf16[128,32,128]{2,0,1:T(8,128)(2,1)S(1)} async-done(((bf16[128,32,128]{2,0,1:T(8,128)(2,1)}), bf16[128,32,128]{2,0,1:T(8,128)(2,1)S(1)}, u32[]{:S(2)}, u32[]{:S(2)}) %all-to-all-start) | async-done | bytes 1048608 | tf_op jit(solution)/shard_map/while/body/eval_jaxpr/all_to_all | solution.py:52
  1074.2 25.0 %collective-permute-done = bf16[128,4096]{0,1:T(8,128)(2,1)S(1)} collective-permute-done((bf16[128,4096]{0,1:T(8,128)(2,1)}, bf16[128,4096]{0,1:T(8,128)(2,1)S(1)}, u32[]{:S(2)}, u32[]{:S(2)}) %collective-permute-start) | collective-permute-done | bytes 1048608 | tf_op jit(solution)/shard_map/while/body/eval_jaxpr/ppermute | solution.py:12
  (576 shorter events, 643.2 us)
Async XLA Ops:
  12.8 24.5 %all-to-all-start = ((bf16[128,32,128]{2,0,1:T(8,128)(2,1)}), bf16[128,32,128]{2,0,1:T(8,128)(2,1)S(1)}, u32[]{:S(2)}, u32[]{:S(2)}) async-start(bf16[128,32,128]{2,0,1:T(8,128)(2,1)} %copy.92), calls=%async_computation | async-start | bytes 2097152 | tf_op jit(solution)/shard_map/while/body/eval_jaxpr/all_to_all | solution.py:52
  78.7 21.9 %all-to-all-start.1 = ((bf16[32,1,128,1,128]{2,4,3,1,0:T(8,128)(2,1)}), bf16[32,1,128,1,128]{2,4,3,1,0:T(8,128)(2,1)}, u32[]{:S(2)}, u32[]{:S(2)}) async-start(bf16[32,1,128,1,128]{2,4,3,1,0:T(8,128)(2,1)} %constant_dynamic-update-slice_fusion.97), calls=%async_computation.1 | async-start | bytes 2097152 | tf_op jit(solution)/shard_map/while/body/eval_jaxpr/all_to_all | solution.py:59
  103.9 28.5 %collective-permute-start = (bf16[128,4096]{0,1:T(8,128)(2,1)}, bf16[128,4096]{0,1:T(8,128)(2,1)S(1)}, u32[]{:S(2)}, u32[]{:S(2)}) collective-permute-start(bf16[128,4096]{0,1:T(8,128)(2,1)} %get-tuple-element.264), channel_id=1, source_target_pairs={{0,32},{32,64},{64,96},{96,128},{128,160},{160,192},{192,224},{1,3... | collective-permute-start | bytes 3145736 | tf_op jit(solution)/shard_map/while/body/eval_jaxpr/ppermute | solution.py:12
  199.5 21.9 %all-to-all-start.1 = ((bf16[32,1,128,1,128]{2,4,3,1,0:T(8,128)(2,1)}), bf16[32,1,128,1,128]{2,4,3,1,0:T(8,128)(2,1)}, u32[]{:S(2)}, u32[]{:S(2)}) async-start(bf16[32,1,128,1,128]{2,4,3,1,0:T(8,128)(2,1)} %constant_dynamic-update-slice_fusion.97), calls=%async_computation.1 | async-start | bytes 2097152 | tf_op jit(solution)/shard_map/while/body/eval_jaxpr/all_to_all | solution.py:59
  224.8 28.5 %collective-permute-start = (bf16[128,4096]{0,1:T(8,128)(2,1)}, bf16[128,4096]{0,1:T(8,128)(2,1)S(1)}, u32[]{:S(2)}, u32[]{:S(2)}) collective-permute-start(bf16[128,4096]{0,1:T(8,128)(2,1)} %get-tuple-element.264), channel_id=1, source_target_pairs={{0,32},{32,64},{64,96},{96,128},{128,160},{160,192},{192,224},{1,3... | collective-permute-start | bytes 3145736 | tf_op jit(solution)/shard_map/while/body/eval_jaxpr/ppermute | solution.py:12
  257.9 21.1 %all-to-all-start = ((bf16[128,32,128]{2,0,1:T(8,128)(2,1)}), bf16[128,32,128]{2,0,1:T(8,128)(2,1)S(1)}, u32[]{:S(2)}, u32[]{:S(2)}) async-start(bf16[128,32,128]{2,0,1:T(8,128)(2,1)} %copy.92), calls=%async_computation | async-start | bytes 2097152 | tf_op jit(solution)/shard_map/while/body/eval_jaxpr/all_to_all | solution.py:52
  320.4 21.9 %all-to-all-start.1 = ((bf16[32,1,128,1,128]{2,4,3,1,0:T(8,128)(2,1)}), bf16[32,1,128,1,128]{2,4,3,1,0:T(8,128)(2,1)}, u32[]{:S(2)}, u32[]{:S(2)}) async-start(bf16[32,1,128,1,128]{2,4,3,1,0:T(8,128)(2,1)} %constant_dynamic-update-slice_fusion.97), calls=%async_computation.1 | async-start | bytes 2097152 | tf_op jit(solution)/shard_map/while/body/eval_jaxpr/all_to_all | solution.py:59
  345.6 28.5 %collective-permute-start = (bf16[128,4096]{0,1:T(8,128)(2,1)}, bf16[128,4096]{0,1:T(8,128)(2,1)S(1)}, u32[]{:S(2)}, u32[]{:S(2)}) collective-permute-start(bf16[128,4096]{0,1:T(8,128)(2,1)} %get-tuple-element.264), channel_id=1, source_target_pairs={{0,32},{32,64},{64,96},{96,128},{128,160},{160,192},{192,224},{1,3... | collective-permute-start | bytes 3145736 | tf_op jit(solution)/shard_map/while/body/eval_jaxpr/ppermute | solution.py:12
  378.7 21.1 %all-to-all-start = ((bf16[128,32,128]{2,0,1:T(8,128)(2,1)}), bf16[128,32,128]{2,0,1:T(8,128)(2,1)S(1)}, u32[]{:S(2)}, u32[]{:S(2)}) async-start(bf16[128,32,128]{2,0,1:T(8,128)(2,1)} %copy.92), calls=%async_computation | async-start | bytes 2097152 | tf_op jit(solution)/shard_map/while/body/eval_jaxpr/all_to_all | solution.py:52
  441.2 21.9 %all-to-all-start.1 = ((bf16[32,1,128,1,128]{2,4,3,1,0:T(8,128)(2,1)}), bf16[32,1,128,1,128]{2,4,3,1,0:T(8,128)(2,1)}, u32[]{:S(2)}, u32[]{:S(2)}) async-start(bf16[32,1,128,1,128]{2,4,3,1,0:T(8,128)(2,1)} %constant_dynamic-update-slice_fusion.97), calls=%async_computation.1 | async-start | bytes 2097152 | tf_op jit(solution)/shard_map/while/body/eval_jaxpr/all_to_all | solution.py:59
  466.5 28.5 %collective-permute-start = (bf16[128,4096]{0,1:T(8,128)(2,1)}, bf16[128,4096]{0,1:T(8,128)(2,1)S(1)}, u32[]{:S(2)}, u32[]{:S(2)}) collective-permute-start(bf16[128,4096]{0,1:T(8,128)(2,1)} %get-tuple-element.264), channel_id=1, source_target_pairs={{0,32},{32,64},{64,96},{96,128},{128,160},{160,192},{192,224},{1,3... | collective-permute-start | bytes 3145736 | tf_op jit(solution)/shard_map/while/body/eval_jaxpr/ppermute | solution.py:12
  499.6 21.1 %all-to-all-start = ((bf16[128,32,128]{2,0,1:T(8,128)(2,1)}), bf16[128,32,128]{2,0,1:T(8,128)(2,1)S(1)}, u32[]{:S(2)}, u32[]{:S(2)}) async-start(bf16[128,32,128]{2,0,1:T(8,128)(2,1)} %copy.92), calls=%async_computation | async-start | bytes 2097152 | tf_op jit(solution)/shard_map/while/body/eval_jaxpr/all_to_all | solution.py:52
  562.1 21.9 %all-to-all-start.1 = ((bf16[32,1,128,1,128]{2,4,3,1,0:T(8,128)(2,1)}), bf16[32,1,128,1,128]{2,4,3,1,0:T(8,128)(2,1)}, u32[]{:S(2)}, u32[]{:S(2)}) async-start(bf16[32,1,128,1,128]{2,4,3,1,0:T(8,128)(2,1)} %constant_dynamic-update-slice_fusion.97), calls=%async_computation.1 | async-start | bytes 2097152 | tf_op jit(solution)/shard_map/while/body/eval_jaxpr/all_to_all | solution.py:59
  587.3 28.5 %collective-permute-start = (bf16[128,4096]{0,1:T(8,128)(2,1)}, bf16[128,4096]{0,1:T(8,128)(2,1)S(1)}, u32[]{:S(2)}, u32[]{:S(2)}) collective-permute-start(bf16[128,4096]{0,1:T(8,128)(2,1)} %get-tuple-element.264), channel_id=1, source_target_pairs={{0,32},{32,64},{64,96},{96,128},{128,160},{160,192},{192,224},{1,3... | collective-permute-start | bytes 3145736 | tf_op jit(solution)/shard_map/while/body/eval_jaxpr/ppermute | solution.py:12
  620.4 21.1 %all-to-all-start = ((bf16[128,32,128]{2,0,1:T(8,128)(2,1)}), bf16[128,32,128]{2,0,1:T(8,128)(2,1)S(1)}, u32[]{:S(2)}, u32[]{:S(2)}) async-start(bf16[128,32,128]{2,0,1:T(8,128)(2,1)} %copy.92), calls=%async_computation | async-start | bytes 2097152 | tf_op jit(solution)/shard_map/while/body/eval_jaxpr/all_to_all | solution.py:52
  682.9 21.9 %all-to-all-start.1 = ((bf16[32,1,128,1,128]{2,4,3,1,0:T(8,128)(2,1)}), bf16[32,1,128,1,128]{2,4,3,1,0:T(8,128)(2,1)}, u32[]{:S(2)}, u32[]{:S(2)}) async-start(bf16[32,1,128,1,128]{2,4,3,1,0:T(8,128)(2,1)} %constant_dynamic-update-slice_fusion.97), calls=%async_computation.1 | async-start | bytes 2097152 | tf_op jit(solution)/shard_map/while/body/eval_jaxpr/all_to_all | solution.py:59
  708.2 28.5 %collective-permute-start = (bf16[128,4096]{0,1:T(8,128)(2,1)}, bf16[128,4096]{0,1:T(8,128)(2,1)S(1)}, u32[]{:S(2)}, u32[]{:S(2)}) collective-permute-start(bf16[128,4096]{0,1:T(8,128)(2,1)} %get-tuple-element.264), channel_id=1, source_target_pairs={{0,32},{32,64},{64,96},{96,128},{128,160},{160,192},{192,224},{1,3... | collective-permute-start | bytes 3145736 | tf_op jit(solution)/shard_map/while/body/eval_jaxpr/ppermute | solution.py:12
  741.3 21.1 %all-to-all-start = ((bf16[128,32,128]{2,0,1:T(8,128)(2,1)}), bf16[128,32,128]{2,0,1:T(8,128)(2,1)S(1)}, u32[]{:S(2)}, u32[]{:S(2)}) async-start(bf16[128,32,128]{2,0,1:T(8,128)(2,1)} %copy.92), calls=%async_computation | async-start | bytes 2097152 | tf_op jit(solution)/shard_map/while/body/eval_jaxpr/all_to_all | solution.py:52
  803.8 21.9 %all-to-all-start.1 = ((bf16[32,1,128,1,128]{2,4,3,1,0:T(8,128)(2,1)}), bf16[32,1,128,1,128]{2,4,3,1,0:T(8,128)(2,1)}, u32[]{:S(2)}, u32[]{:S(2)}) async-start(bf16[32,1,128,1,128]{2,4,3,1,0:T(8,128)(2,1)} %constant_dynamic-update-slice_fusion.97), calls=%async_computation.1 | async-start | bytes 2097152 | tf_op jit(solution)/shard_map/while/body/eval_jaxpr/all_to_all | solution.py:59
  829.0 28.5 %collective-permute-start = (bf16[128,4096]{0,1:T(8,128)(2,1)}, bf16[128,4096]{0,1:T(8,128)(2,1)S(1)}, u32[]{:S(2)}, u32[]{:S(2)}) collective-permute-start(bf16[128,4096]{0,1:T(8,128)(2,1)} %get-tuple-element.264), channel_id=1, source_target_pairs={{0,32},{32,64},{64,96},{96,128},{128,160},{160,192},{192,224},{1,3... | collective-permute-start | bytes 3145736 | tf_op jit(solution)/shard_map/while/body/eval_jaxpr/ppermute | solution.py:12
  924.6 21.9 %all-to-all-start.1 = ((bf16[32,1,128,1,128]{2,4,3,1,0:T(8,128)(2,1)}), bf16[32,1,128,1,128]{2,4,3,1,0:T(8,128)(2,1)}, u32[]{:S(2)}, u32[]{:S(2)}) async-start(bf16[32,1,128,1,128]{2,4,3,1,0:T(8,128)(2,1)} %constant_dynamic-update-slice_fusion.97), calls=%async_computation.1 | async-start | bytes 2097152 | tf_op jit(solution)/shard_map/while/body/eval_jaxpr/all_to_all | solution.py:59
  949.9 28.5 %collective-permute-start = (bf16[128,4096]{0,1:T(8,128)(2,1)}, bf16[128,4096]{0,1:T(8,128)(2,1)S(1)}, u32[]{:S(2)}, u32[]{:S(2)}) collective-permute-start(bf16[128,4096]{0,1:T(8,128)(2,1)} %get-tuple-element.264), channel_id=1, source_target_pairs={{0,32},{32,64},{64,96},{96,128},{128,160},{160,192},{192,224},{1,3... | collective-permute-start | bytes 3145736 | tf_op jit(solution)/shard_map/while/body/eval_jaxpr/ppermute | solution.py:12
  1045.5 21.9 %all-to-all-start.1 = ((bf16[32,1,128,1,128]{2,4,3,1,0:T(8,128)(2,1)}), bf16[32,1,128,1,128]{2,4,3,1,0:T(8,128)(2,1)}, u32[]{:S(2)}, u32[]{:S(2)}) async-start(bf16[32,1,128,1,128]{2,4,3,1,0:T(8,128)(2,1)} %constant_dynamic-update-slice_fusion.97), calls=%async_computation.1 | async-start | bytes 2097152 | tf_op jit(solution)/shard_map/while/body/eval_jaxpr/all_to_all | solution.py:59
  1070.7 28.5 %collective-permute-start = (bf16[128,4096]{0,1:T(8,128)(2,1)}, bf16[128,4096]{0,1:T(8,128)(2,1)S(1)}, u32[]{:S(2)}, u32[]{:S(2)}) collective-permute-start(bf16[128,4096]{0,1:T(8,128)(2,1)} %get-tuple-element.264), channel_id=1, source_target_pairs={{0,32},{32,64},{64,96},{96,128},{128,160},{160,192},{192,224},{1,3... | collective-permute-start | bytes 3145736 | tf_op jit(solution)/shard_map/while/body/eval_jaxpr/ppermute | solution.py:12
  (4 other events, 65.1 us)
